TPU v7x, 32 devices: a whole 2x2x4 slice. The times are simulated.
32 devices in a mesh: groups: 2 (over y), ctx: 8 (over z, x), mp: 2 (over core).
Axes of the slice: x: 2, y: 2, z: 4, core: 2. Of those that a mesh axis runs over, the one named last changes fastest.
Arguments:
- inputs: bfloat16 [2048, 2048], P(('groups', 'ctx'), 'mp'), parts along dimension 0, may hold values from -6 to 6
- cotangent: bfloat16 [2048, 2048], P(('groups', 'ctx'), 'mp'), parts along dimension 0, may hold values from -0.1875 to 0.1875
- filters: float32 [1024, 24], P('ctx'), may hold values from -0.1875 to 0.1875
- mixing: float32 [24, 2048], P(None, 'mp'), may hold values from -1.25 to 1.25
- ar_coef: float32 [3, 2048], P(None, 'mp'), may hold values from -3 to 3
Outputs:
- outputs: bfloat16 [2048, 2048], P(('groups', 'ctx'), 'mp'), parts along dimension 0
- grad_mixing: float32 [48, 2048], P('groups', 'mp'), parts along dimension 0
- grad_ar: float32 [6, 2048], P('groups', 'mp'), parts along dimension 0
There are 2 independent parts, one for each index of `groups`. A program takes and returns all parts, laid end to end along the dimension named above; an argument that names none is the same for every part. Nothing has to cross between parts.
All inputs are finite; a program needn't handle non-finite values.
Results may differ from a plain program's by a relative error of at most 0.001.
Values may be sent and summed in bfloat16 or wider, within the bound.
No kernel may reach another device: no remote copies, remote signals or barrier semaphores. Data moves between devices by JAX's collectives and lax.ppermute only.
A program may use at most 64 MiB of HBM per device.

v0:
```python
import math
import jax
import jax.numpy as jnp
from jax import lax
from jax.sharding import PartitionSpec as P

ORDER = 3
highest = lax.Precision.HIGHEST


def phase_tables(seq_len):
    radix_len = math.gcd(seq_len, 128)
    outer_len = 2 * seq_len // radix_len
    half_outer = outer_len // 2
    total_len = 2 * seq_len
    low_index = jnp.arange(half_outer, dtype=jnp.int32)
    outer_index = jnp.arange(outer_len, dtype=jnp.int32)
    radix_index = jnp.arange(radix_len, dtype=jnp.int32)
    outer_angle = (low_index[:, None] * outer_index[None, :] % outer_len).astype(jnp.float32) * (
        2.0 * math.pi / outer_len
    )
    twist_angle = (outer_index[:, None] * radix_index[None, :] % total_len).astype(jnp.float32) * (
        2.0 * math.pi / total_len
    )
    radix_angle = (radix_index[:, None] * radix_index[None, :] % radix_len).astype(jnp.float32) * (
        2.0 * math.pi / radix_len
    )
    return (
        jnp.cos(outer_angle),
        jnp.sin(outer_angle),
        jnp.cos(twist_angle),
        jnp.sin(twist_angle),
        jnp.cos(radix_angle),
        jnp.sin(radix_angle),
    )


def forward_spectrum(signal, tables):
    outer_cos, outer_sin, twist_cos, twist_sin, radix_cos, radix_sin = tables
    channels = signal.shape[0]
    folded = signal.reshape(channels, outer_cos.shape[0], radix_cos.shape[0])
    first_real = jnp.einsum("chr,hk->ckr", folded, outer_cos, precision=highest)
    first_imag = -jnp.einsum("chr,hk->ckr", folded, outer_sin, precision=highest)
    turned_real = first_real * twist_cos + first_imag * twist_sin
    turned_imag = first_imag * twist_cos - first_real * twist_sin
    spec_real = jnp.einsum("ckr,rq->ckq", turned_real, radix_cos, precision=highest) + jnp.einsum(
        "ckr,rq->ckq", turned_imag, radix_sin, precision=highest
    )
    spec_imag = jnp.einsum("ckr,rq->ckq", turned_imag, radix_cos, precision=highest) - jnp.einsum(
        "ckr,rq->ckq", turned_real, radix_sin, precision=highest
    )
    return (spec_real, spec_imag)


def inverse_spectrum(spec_real, spec_imag, tables):
    outer_cos, outer_sin, twist_cos, twist_sin, radix_cos, radix_sin = tables
    back_real = jnp.einsum("ckq,rq->ckr", spec_real, radix_cos, precision=highest) - jnp.einsum(
        "ckq,rq->ckr", spec_imag, radix_sin, precision=highest
    )
    back_imag = jnp.einsum("ckq,rq->ckr", spec_real, radix_sin, precision=highest) + jnp.einsum(
        "ckq,rq->ckr", spec_imag, radix_cos, precision=highest
    )
    untwist_real = back_real * twist_cos - back_imag * twist_sin
    untwist_imag = back_real * twist_sin + back_imag * twist_cos
    folded = jnp.einsum("ckr,hk->chr", untwist_real, outer_cos, precision=highest) - jnp.einsum(
        "ckr,hk->chr", untwist_imag, outer_sin, precision=highest
    )
    channels = folded.shape[0]
    total_len = 2 * folded.shape[1] * folded.shape[2]
    return folded.reshape(channels, -1) / total_len


def local(inputs, cotangent, filters, mixing, ar_coef):
    tok_rows, local_width = inputs.shape
    ctx_count = lax.axis_size("ctx")
    ctx_place = lax.axis_index("ctx")
    narrow = local_width // ctx_count
    seq_len = tok_rows * ctx_count
    tables = phase_tables(seq_len)
    seq_cols = lax.all_to_all(inputs.T, "ctx", split_axis=0, concat_axis=1, tiled=True)
    signal = seq_cols.astype(jnp.float32)
    filter_all = lax.all_gather(filters, "ctx", axis=0, tiled=True)
    mix_local = lax.dynamic_slice_in_dim(mixing, ctx_place * narrow, narrow, 1)
    kernel = jnp.einsum("lk,kc->cl", filter_all, mix_local, precision=highest)
    sig_real, sig_imag = forward_spectrum(signal, tables)
    ker_real, ker_imag = forward_spectrum(kernel, tables)
    convolved = inverse_spectrum(
        ker_real * sig_real - ker_imag * sig_imag, ker_real * sig_imag + ker_imag * sig_real, tables
    )
    cot_cols = lax.all_to_all(cotangent.T, "ctx", split_axis=0, concat_axis=1, tiled=True)
    cot_real, cot_imag = forward_spectrum(cot_cols.astype(jnp.float32), tables)
    lagged = inverse_spectrum(
        cot_real * sig_real + cot_imag * sig_imag, cot_imag * sig_real - cot_real * sig_imag, tables
    )
    ar_local = lax.dynamic_slice_in_dim(ar_coef, ctx_place * narrow, narrow, 1)
    padded = jnp.pad(signal, ((0, 0), (ORDER, 0)))
    autoreg = jnp.zeros_like(signal)
    for lag_step in range(1, ORDER + 1):
        autoreg = (
            autoreg
            + ar_local[lag_step - 1][:, None]
            * padded[:, ORDER - lag_step : ORDER - lag_step + seq_len]
        )
    out_cols = (convolved + autoreg).astype(jnp.bfloat16)
    outputs = lax.all_to_all(out_cols, "ctx", split_axis=1, concat_axis=0, tiled=True).T
    mix_piece = jnp.einsum("lk,cl->kc", filter_all, lagged, precision=highest)
    grad_mixing, grad_ar = (
        lax.all_gather(mix_piece, "ctx", axis=1, tiled=True),
        lax.all_gather(lagged[:, 1 : ORDER + 1].T, "ctx", axis=1, tiled=True),
    )
    return (outputs, grad_mixing, grad_ar)


def solution(mesh):
    return jax.shard_map(
        local,
        mesh=mesh,
        in_specs=(
            P(("groups", "ctx"), "mp"),
            P(("groups", "ctx"), "mp"),
            P("ctx", None),
            P(None, "mp"),
            P(None, "mp"),
        ),
        out_specs=(P(("groups", "ctx"), "mp"), P("groups", "mp"), P("groups", "mp")),
        check_vma=False,
    )
```

profile of v0, /device:TPU:0, one launch (start us, length us, event | category | flops | bytes accessed | tf_op | source)
XLA Modules:
  0.0 162.7 jit_solution(16318002603742689494)
XLA Ops:
  0.6 1.8 %copy.72 = bf16[128,1024]{0,1:T(8,128)(2,1)} copy(bf16[128,1024]{1,0:T(8,128)(2,1)} %param.5) | data formatting | bytes 524288 | tf_op args[0]
  2.5 7.3 %all-to-all-start = ((bf16[8,128,128]{2,1,0:T(8,128)(2,1)}), bf16[8,128,128]{2,1,0:T(8,128)(2,1)S(1)}, u32[]{:S(2)}, u32[]{:S(2)}) async-start(bf16[8,128,128]{2,1,0:T(8,128)(2,1)} %bitcast.7), calls=%async_computation | async-start | bytes 524288 | tf_op jit(solution)/shard_map/all_to_all | solution.py:80
  10.5 32.3 %all_gather.9 = f32[1024,24]{0,1:T(8,128)S(1)} all-gather(f32[128,24]{0,1:T(8,128)S(1)} %copy-done.3), channel_id=1, replica_groups=mesh['groups'=2,'ctx'=8,'mp'=2] {'ctx'}, dimensions={0}, use_global_device_ids=true | all-gather | bytes 110592 | tf_op jit(solution)/shard_map/all_gather | solution.py:82
  45.9 2.1 %convolution_negate_fusion = f32[16,128,128]{2,0,1:T(8,128)} fusion(f32[128,8,128]{2,1,0:T(8,128)S(1)} %bitcast.144), kind=kOutput, calls=%fused_computation | convolution fusion | flops 25429760 | bytes 1572864 | tf_op jit(solution)/shard_map/chr,hk->ckr/dot_general | solution.py:43
  47.9 4.8 %all-to-all-start.2 = ((bf16[8,128,128]{2,1,0:T(8,128)(2,1)}), bf16[8,128,128]{2,1,0:T(8,128)(2,1)S(1)}, u32[]{:S(2)}, u32[]{:S(2)}) async-start(bf16[8,128,128]{2,1,0:T(8,128)(2,1)} %bitcast.20), calls=%async_computation.2 | async-start | bytes 524288 | tf_op jit(solution)/shard_map/all_to_all | solution.py:90
  54.1 6.3 %all-to-all-done.2 = bf16[8,128,128]{2,1,0:T(8,128)(2,1)S(1)} async-done(((bf16[8,128,128]{2,1,0:T(8,128)(2,1)}), bf16[8,128,128]{2,1,0:T(8,128)(2,1)S(1)}, u32[]{:S(2)}, u32[]{:S(2)}) %all-to-all-start.2) | async-done | bytes 262176 | tf_op jit(solution)/shard_map/all_to_all | solution.py:90
  61.8 1.9 %add_bitcast_fusion = (f32[128,16,128]{2,1,0:T(8,128)S(1)}, f32[128,16,128]{2,1,0:T(8,128)S(1)}, f32[128,16,128]{2,1,0:T(8,128)S(1)}, f32[128,16,128]{2,1,0:T(8,...) fusion(f32[16,128,128]{2,0,1:T(8,128)S(1)} %convolution_negate_fusion.1, ...), kind=kOutput, calls=%fused_computation.30 | convolution fusion | flops 29886208 | bytes 12075008 | tf_op jit(solution)/shard_map/chr,hk->ckr/dot_general | solution.py:42
  63.7 1.4 fusion.24
  65.1 1.4 fusion.20
  66.6 1.4 convolution_add_fusion.4
  68.0 1.4 convolution_subtract_fusion.4
  69.5 1.4 fusion.18
  70.9 1.6 fusion.14
  72.5 1.4 convolution_add_fusion.3
  73.9 1.4 fusion.8
  75.4 1.4 fusion.12
  76.8 1.4 convolution_subtract_fusion.1
  78.3 1.4 convolution_subtract_fusion.3
  79.7 1.8 %multiply_subtract_fusion.1 = (f32[128,16,128]{2,0,1:T(8,128)S(1)}, f32[128,16,128]{2,0,1:T(8,128)S(1)}, f32[128,16,128]{2,0,1:T(8,128)S(1)}, f32[128,16,128]{2,0,1:T(8,128)S(1)}) fusion(f32[128,16,128]{2,0,1:T(8,128)S(1)} %convolution_subtract_fusion.3, f32[128,16,128]{2,0,1:T(8,128)S(1)} %convolution_subtract_fusion.1, ...), kind=kOutput, calls=%fused_computation.27 | convolution fusion | flops 406290432 | bytes 11534336 | tf_op jit(solution)/shard_map/ckr,rq->ckq/dot_general | solution.py:46
  81.5 1.2 fusion.58
  82.7 1.5 fusion.45
  84.2 1.2 fusion.53
  85.4 1.2 fusion.40
  86.7 1.3 convolution_subtract_fusion.2
  87.9 1.2 convolution_add_fusion.2
  89.2 1.2 convolution_subtract_fusion
  90.5 1.7 %multiply_add_fusion = (f32[128,16,128]{2,0,1:T(8,128)S(1)}, f32[128,16,128]{2,0,1:T(8,128)S(1)}, f32[128,16,128]{2,0,1:T(8,128)S(1)}, f32[128,16,128]{2,0,1:T(8,128)S(1)}) fusion(f32[128,16,128]{2,0,1:T(8,128)S(1)} %convolution_subtract_fusion, f32[16,128]{1,0:T(8,128)S(1)} %get-tuple-element.31, f32[16,128]{1,0:T(8,128)S(1)} %get-tuple-element.32, ...), kind=kOutput, calls=%fused_computation.25 | convolution fusion | flops 406290432 | bytes 9453568 | tf_op jit(solution)/shard_map/ckq,rq->ckr/dot_general | solution.py:60
  94.9 1.4 fusion.1
  97.6 3.4 %all-to-all-start.1 = ((bf16[128,8,128]{0,2,1:T(8,128)(2,1)}), bf16[128,8,128]{0,2,1:T(8,128)(2,1)S(1)}, u32[]{:S(2)}, u32[]{:S(2)}) async-start(bf16[128,8,128]{0,2,1:T(8,128)(2,1)} %bitcast.15), calls=%async_computation.1 | async-start | bytes 524288 | tf_op jit(solution)/shard_map/all_to_all | solution.py:105
  101.0 1.2 fusion
  102.5 26.6 %all_gather.11 = f32[3,1024]{1,0:T(4,128)S(1)} all-gather(f32[3,128]{1,0:T(4,128)S(1)} %bitcast.153), channel_id=1, replica_groups=mesh['groups'=2,'ctx'=8,'mp'=2] {'ctx'}, dimensions={1}, use_global_device_ids=true | all-gather | bytes 13824 | tf_op jit(solution)/shard_map/all_gather | solution.py:109
  129.6 30.6 %all_gather.10 = f32[24,1024]{1,0:T(8,128)S(1)} all-gather(f32[24,128]{1,0:T(8,128)S(1)} %convolution_bitcast_fusion.1), channel_id=1, replica_groups=mesh['groups'=2,'ctx'=8,'mp'=2] {'ctx'}, dimensions={1}, use_global_device_ids=true | all-gather | bytes 110592 | tf_op jit(solution)/shard_map/all_gather | solution.py:108
  (35 shorter events, 13.5 us)
Async XLA Ops:
  0.6 42.1 %copy-start = (f32[24,1024]{1,0:T(8,128)S(1)}, f32[24,1024]{1,0:T(8,128)}, u32[]{:S(2)}) copy-start(f32[24,1024]{1,0:T(8,128)} %param.8) | copy-start | bytes 294916
  2.5 45.4 %all-to-all-start = ((bf16[8,128,128]{2,1,0:T(8,128)(2,1)}), bf16[8,128,128]{2,1,0:T(8,128)(2,1)S(1)}, u32[]{:S(2)}, u32[]{:S(2)}) async-start(bf16[8,128,128]{2,1,0:T(8,128)(2,1)} %bitcast.7), calls=%async_computation | async-start | bytes 524288 | tf_op jit(solution)/shard_map/all_to_all | solution.py:80
  9.8 0.7 copy-start.3
  43.4 1.0 copy-start.2
  47.9 12.5 %all-to-all-start.2 = ((bf16[8,128,128]{2,1,0:T(8,128)(2,1)}), bf16[8,128,128]{2,1,0:T(8,128)(2,1)S(1)}, u32[]{:S(2)}, u32[]{:S(2)}) async-start(bf16[8,128,128]{2,1,0:T(8,128)(2,1)} %bitcast.20), calls=%async_computation.2 | async-start | bytes 524288 | tf_op jit(solution)/shard_map/all_to_all | solution.py:90
  60.4 1.4 copy-start.1
  97.6 62.6 %all-to-all-start.1 = ((bf16[128,8,128]{0,2,1:T(8,128)(2,1)}), bf16[128,8,128]{0,2,1:T(8,128)(2,1)S(1)}, u32[]{:S(2)}, u32[]{:S(2)}) async-start(bf16[128,8,128]{0,2,1:T(8,128)(2,1)} %bitcast.15), calls=%async_computation.1 | async-start | bytes 524288 | tf_op jit(solution)/shard_map/all_to_all | solution.py:105
where the time goes:
time: 166 us; the launch traced here: 163 us
  blocking collectives  89.5 us (54%)
  matrix products  41.1 us (25%)
  starting transfers between devices  15.5 us (9%)
  local copies, waits for them, and re-layouts  8.53 us (5%)
  waiting for transfers between devices  6.35 us (4%)
    all_gather x1, blocking collectives, local(): filter_all = lax.all_gather(filters, 'ctx', axis=0, tiled=True)  32.3 us
    all_gather x1, blocking collectives, local(): lax.all_gather(mix_piece, 'ctx', axis=1, tiled=True)  30.6 us
    all_gather x1, blocking collectives, local(): lax.all_gather(lagged[:, 1:ORDER + 1].T, 'ctx', axis=1, tiled=True)  26.6 us
    all_to_all x1, starting transfers between devices, local(): lax.all_to_all(inputs.T, 'ctx', split_axis=0, concat_axis=1, tiled=True)  7.28 us
    unnamed x17, local copies, waits for them, and re-layouts  6.57 us
    all_to_all x1, waiting for transfers between devices, local(): lax.all_to_all(cotangent.T, 'ctx', split_axis=0, concat_axis=1, tiled=True)  6.34 us
    all_to_all x1, starting transfers between devices, local(): lax.all_to_all(cotangent.T, 'ctx', split_axis=0, concat_axis=1, tiled=True)  4.76 us
    dot_general x3, matrix products, forward_spectrum(): jnp.einsum('ckr,rq->ckq', turned_imag, radix_sin, precision=highest)  4.67 us
  transfers between devices with their start and end apart: 3, of which 1 were waited for; matrix products, arithmetic and copies ran while one was open for 5% of the time, Pallas kernels for 0%

commit v1 on v0

--- a/solution.py
+++ b/solution.py
@@ -6,6 +6,24 @@
 
 ORDER = 3
 highest = lax.Precision.HIGHEST
+
+
+def collect(value, axis, dim):
+    ways, here, step = (lax.axis_size(axis), lax.axis_index(axis), value.shape[dim])
+    dims = [n * ways if d == dim else n for d, n in enumerate(value.shape)]
+    full = lax.dynamic_update_slice_in_dim(
+        jnp.zeros(dims, value.dtype), value, here * step, axis=dim
+    )
+    going_up = going_down = value
+    for far in range(1, ways // 2 + 1):
+        going_up = lax.ppermute(going_up, axis, [(d, (d + 1) % ways) for d in range(ways)])
+        full = lax.dynamic_update_slice_in_dim(full, going_up, (here - far) % ways * step, axis=dim)
+        if 2 * far < ways:
+            going_down = lax.ppermute(going_down, axis, [(d, (d - 1) % ways) for d in range(ways)])
+            full = lax.dynamic_update_slice_in_dim(
+                full, going_down, (here + far) % ways * step, axis=dim
+            )
+    return full
 
 
 def phase_tables(seq_len):
@@ -105,7 +123,7 @@
     outputs = lax.all_to_all(out_cols, "ctx", split_axis=1, concat_axis=0, tiled=True).T
     mix_piece = jnp.einsum("lk,cl->kc", filter_all, lagged, precision=highest)
     grad_mixing, grad_ar = (
-        lax.all_gather(mix_piece, "ctx", axis=1, tiled=True),
+        collect(mix_piece, "ctx", 1),
         lax.all_gather(lagged[:, 1 : ORDER + 1].T, "ctx", axis=1, tiled=True),
     )
     return (outputs, grad_mixing, grad_ar)

time: 166 us -> 161 us (0.970)
  blocking collectives: 89.5 us -> 58.2 us
  starting transfers between devices: 15.5 us -> 30.1 us
  waiting for transfers between devices: 6.35 us -> 18.2 us
    all_gather x1 -> x0, blocking collectives: 30.6 us -> none  [local(): lax.all_gather(mix_piece, 'ctx', axis=1, tiled=True)]
    ppermute x0 -> x7, starting transfers between devices: none -> 14.5 us  [the longest x3 12.5 us: collect(): lax.ppermute(going_down, axis, [(d, (d - 1) % ways) for d in range(ways)])]
    ppermute x0 -> x7, waiting for transfers between devices: none -> 11.9 us  [the longest x4 11.9 us: collect(): lax.ppermute(going_up, axis, [(d, (d + 1) % ways) for d in range(ways)])]
    unnamed x17 -> x18, local copies, waits for them, and re-layouts: 6.57 us -> 6.39 us
  transfers between devices with their start and end apart: 3 -> 10, of which waited for: 1 -> 4; matrix products, arithmetic and copies ran while one was open for 5% -> 6% of each run, Pallas kernels for 0% -> 0%
where the time goes in v1:
time: 161 us; the launch traced here: 158 us
  blocking collectives  58.2 us (36%)
  matrix products  40.9 us (25%)
  starting transfers between devices  30.1 us (19%)
  waiting for transfers between devices  18.2 us (11%)
  local copies, waits for them, and re-layouts  8.39 us (5%)
    all_gather x1, blocking collectives, local(): filter_all = lax.all_gather(filters, 'ctx', axis=0, tiled=True)  32.1 us
    all_gather x1, blocking collectives, local(): lax.all_gather(lagged[:, 1:ORDER + 1].T, 'ctx', axis=1, tiled=True)  26.1 us
    ppermute x3, starting transfers between devices, collect(): lax.ppermute(going_down, axis, [(d, (d - 1) % ways) for d in range(ways)])  12.5 us
    ppermute x4, waiting for transfers between devices, collect(): lax.ppermute(going_up, axis, [(d, (d + 1) % ways) for d in range(ways)])  11.9 us
    all_to_all x1, starting transfers between devices, local(): lax.all_to_all(inputs.T, 'ctx', split_axis=0, concat_axis=1, tiled=True)  7.28 us
    unnamed x18, local copies, waits for them, and re-layouts  6.39 us
    all_to_all x1, waiting for transfers between devices, local(): lax.all_to_all(cotangent.T, 'ctx', split_axis=0, concat_axis=1, tiled=True)  6.34 us
    all_to_all x1, starting transfers between devices, local(): lax.all_to_all(cotangent.T, 'ctx', split_axis=0, concat_axis=1, tiled=True)  4.93 us
  transfers between devices with their start and end apart: 10, of which 4 were waited for; matrix products, arithmetic and copies ran while one was open for 6% of the time, Pallas kernels for 0%

profile of v1, /device:TPU:0, one launch (start us, length us, event | category | flops | bytes accessed | tf_op | source)
XLA Modules:
  0.0 157.8 jit_solution(8714637921328216467)
XLA Ops:
  0.6 1.8 %copy.72 = bf16[128,1024]{0,1:T(8,128)(2,1)} copy(bf16[128,1024]{1,0:T(8,128)(2,1)} %param.5) | data formatting | bytes 524288 | tf_op args[0]
  2.5 7.3 %all-to-all-start = ((bf16[8,128,128]{2,1,0:T(8,128)(2,1)}), bf16[8,128,128]{2,1,0:T(8,128)(2,1)S(1)}, u32[]{:S(2)}, u32[]{:S(2)}) async-start(bf16[8,128,128]{2,1,0:T(8,128)(2,1)} %bitcast.7), calls=%async_computation | async-start | bytes 524288 | tf_op jit(solution)/shard_map/all_to_all | solution.py:98
  10.6 32.1 %all_gather.6 = f32[1024,24]{0,1:T(8,128)S(1)} all-gather(f32[128,24]{0,1:T(8,128)S(1)} %copy-done.4), channel_id=1, replica_groups=mesh['groups'=2,'ctx'=8,'mp'=2] {'ctx'}, dimensions={0}, use_global_device_ids=true | all-gather | bytes 110592 | tf_op jit(solution)/shard_map/all_gather | solution.py:100
  45.8 2.1 %convolution_negate_fusion = f32[16,128,128]{2,0,1:T(8,128)} fusion(f32[128,8,128]{2,1,0:T(8,128)S(1)} %bitcast.146), kind=kOutput, calls=%fused_computation | convolution fusion | flops 25429760 | bytes 1572864 | tf_op jit(solution)/shard_map/chr,hk->ckr/dot_general | solution.py:61
  47.9 4.9 %all-to-all-start.2 = ((bf16[8,128,128]{2,1,0:T(8,128)(2,1)}), bf16[8,128,128]{2,1,0:T(8,128)(2,1)S(1)}, u32[]{:S(2)}, u32[]{:S(2)}) async-start(bf16[8,128,128]{2,1,0:T(8,128)(2,1)} %bitcast.20), calls=%async_computation.2 | async-start | bytes 524288 | tf_op jit(solution)/shard_map/all_to_all | solution.py:108
  54.2 6.3 %all-to-all-done.2 = bf16[8,128,128]{2,1,0:T(8,128)(2,1)S(1)} async-done(((bf16[8,128,128]{2,1,0:T(8,128)(2,1)}), bf16[8,128,128]{2,1,0:T(8,128)(2,1)S(1)}, u32[]{:S(2)}, u32[]{:S(2)}) %all-to-all-start.2) | async-done | bytes 262176 | tf_op jit(solution)/shard_map/all_to_all | solution.py:108
  61.9 1.9 %add_bitcast_fusion = (f32[128,16,128]{2,1,0:T(8,128)S(1)}, f32[128,16,128]{2,1,0:T(8,128)S(1)}, f32[128,16,128]{2,1,0:T(8,128)S(1)}, f32[128,16,128]{2,1,0:T(8,...) fusion(f32[16,128,128]{2,0,1:T(8,128)S(1)} %convolution_negate_fusion.1, ...), kind=kOutput, calls=%fused_computation.30 | convolution fusion | flops 29886208 | bytes 12075008 | tf_op jit(solution)/shard_map/chr,hk->ckr/dot_general | solution.py:60
  63.9 1.4 fusion.24
  65.3 1.4 fusion.20
  66.7 1.4 convolution_add_fusion.4
  68.2 1.4 convolution_subtract_fusion.4
  69.6 1.4 fusion.18
  71.0 1.6 %fusion.14 = f32[128,16,128]{2,0,1:T(8,128)S(1)} fusion(f32[128,16,128]{2,1,0:T(8,128)S(1)} %get-tuple-element.24), kind=kOutput, calls=%fused_computation.45 | convolution fusion | flops 402882560 | bytes 2097152 | tf_op jit(solution)/shard_map/ckr,rq->ckq/dot_general | solution.py:67
  72.6 1.4 convolution_add_fusion.3
  74.1 1.4 fusion.8
  75.5 1.4 fusion.12
  77.0 1.4 convolution_subtract_fusion.1
  78.4 1.4 convolution_subtract_fusion.3
  79.9 1.8 %multiply_subtract_fusion.1 = (f32[128,16,128]{2,0,1:T(8,128)S(1)}, f32[128,16,128]{2,0,1:T(8,128)S(1)}, f32[128,16,128]{2,0,1:T(8,128)S(1)}, f32[128,16,128]{2,0,1:T(8,128)S(1)}) fusion(f32[128,16,128]{2,0,1:T(8,128)S(1)} %convolution_subtract_fusion.3, f32[128,16,128]{2,0,1:T(8,128)S(1)} %convolution_subtract_fusion.1, ...), kind=kOutput, calls=%fused_computation.27 | convolution fusion | flops 406290432 | bytes 11534336 | tf_op jit(solution)/shard_map/ckr,rq->ckq/dot_general | solution.py:64
  82.9 1.5 fusion.45
  86.9 1.3 convolution_subtract_fusion.2
  89.4 1.2 convolution_subtract_fusion
  90.6 1.7 %multiply_add_fusion = (f32[128,16,128]{2,0,1:T(8,128)S(1)}, f32[128,16,128]{2,0,1:T(8,128)S(1)}, f32[128,16,128]{2,0,1:T(8,128)S(1)}, f32[128,16,128]{2,0,1:T(8,128)S(1)}) fusion(f32[128,16,128]{2,0,1:T(8,128)S(1)} %convolution_subtract_fusion, f32[16,128]{1,0:T(8,128)S(1)} %get-tuple-element.33, f32[16,128]{1,0:T(8,128)S(1)} %get-tuple-element.34, ...), kind=kOutput, calls=%fused_computation.25 | convolution fusion | flops 406290432 | bytes 9453568 | tf_op jit(solution)/shard_map/ckq,rq->ckr/dot_general | solution.py:78
  95.3 4.9 %collective-permute-start.1 = (f32[24,128]{1,0:T(8,128)S(1)}, f32[24,128]{1,0:T(8,128)S(1)}, u32[]{:S(2)}, u32[]{:S(2)}) collective-permute-start(f32[24,128]{1,0:T(8,128)S(1)} %get-tuple-element.32), channel_id=1, source_target_pairs={{0,14},{2,0},{4,2},{6,4},{8,6},{10,8},{12,10},{14,12},{1,15},{3,1}... | collective-permute-start | bytes 36872 | tf_op jit(solution)/shard_map/ppermute | solution.py:22
  103.6 26.1 %all_gather.7 = f32[3,1024]{1,0:T(4,128)S(1)} all-gather(f32[3,128]{1,0:T(4,128)S(1)} %bitcast.155), channel_id=1, replica_groups=mesh['groups'=2,'ctx'=8,'mp'=2] {'ctx'}, dimensions={1}, use_global_device_ids=true | all-gather | bytes 13824 | tf_op jit(solution)/shard_map/all_gather | solution.py:127
  130.6 3.4 %all-to-all-start.1 = ((bf16[128,8,128]{0,2,1:T(8,128)(2,1)}), bf16[128,8,128]{0,2,1:T(8,128)(2,1)S(1)}, u32[]{:S(2)}, u32[]{:S(2)}) async-start(bf16[128,8,128]{0,2,1:T(8,128)(2,1)} %bitcast.15), calls=%async_computation.1 | async-start | bytes 524288 | tf_op jit(solution)/shard_map/all_to_all | solution.py:123
  134.0 1.9 %collective-permute-start.2 = (f32[24,128]{1,0:T(8,128)S(1)}, f32[24,128]{1,0:T(8,128)S(1)}, u32[]{:S(2)}, u32[]{:S(2)}) collective-permute-start(f32[24,128]{1,0:T(8,128)S(1)} %collective-permute-done), channel_id=1, source_target_pairs={{0,2},{2,4},{4,6},{6,8},{8,10},{10,12},{12,14},{14,0},{1,3},{3,5},... | collective-permute-start | bytes 36872 | tf_op jit(solution)/shard_map/ppermute | solution.py:19
  136.0 2.9 %collective-permute-start.3 = (f32[24,128]{1,0:T(8,128)S(1)}, f32[24,128]{1,0:T(8,128)S(1)}, u32[]{:S(2)}, u32[]{:S(2)}) collective-permute-start(f32[24,128]{1,0:T(8,128)S(1)} %collective-permute-done.1), channel_id=1, source_target_pairs={{0,14},{2,0},{4,2},{6,4},{8,6},{10,8},{12,10},{14,12},{1,15},{3,1}... | collective-permute-start | bytes 36872 | tf_op jit(solution)/shard_map/ppermute | solution.py:22
  138.8 3.8 %collective-permute-done.2 = f32[24,128]{1,0:T(8,128)S(1)} collective-permute-done((f32[24,128]{1,0:T(8,128)S(1)}, f32[24,128]{1,0:T(8,128)S(1)}, u32[]{:S(2)}, u32[]{:S(2)}) %collective-permute-start.2) | collective-permute-done | bytes 12320 | tf_op jit(solution)/shard_map/ppermute | solution.py:19
  142.7 4.7 %collective-permute-start.5 = (f32[24,128]{1,0:T(8,128)S(1)}, f32[24,128]{1,0:T(8,128)S(1)}, u32[]{:S(2)}, u32[]{:S(2)}) collective-permute-start(f32[24,128]{1,0:T(8,128)S(1)} %collective-permute-done.3), channel_id=1, source_target_pairs={{0,14},{2,0},{4,2},{6,4},{8,6},{10,8},{12,10},{14,12},{1,15},{3,1}... | collective-permute-start | bytes 36872 | tf_op jit(solution)/shard_map/ppermute | solution.py:22
  147.4 1.7 %collective-permute-done.4 = f32[24,128]{1,0:T(8,128)S(1)} collective-permute-done((f32[24,128]{1,0:T(8,128)S(1)}, f32[24,128]{1,0:T(8,128)S(1)}, u32[]{:S(2)}, u32[]{:S(2)}) %collective-permute-start.4) | collective-permute-done | bytes 12320 | tf_op jit(solution)/shard_map/ppermute | solution.py:19
  149.1 6.4 %collective-permute-done.6 = f32[24,128]{1,0:T(8,128)S(1)} collective-permute-done((f32[24,128]{1,0:T(8,128)S(1)}, f32[24,128]{1,0:T(8,128)S(1)}, u32[]{:S(2)}, u32[]{:S(2)}) %collective-permute-start.6) | collective-permute-done | bytes 12320 | tf_op jit(solution)/shard_map/ppermute | solution.py:19
  (57 shorter events, 20.8 us)
Async XLA Ops:
  0.6 42.1 %copy-start = (f32[24,1024]{1,0:T(8,128)S(1)}, f32[24,1024]{1,0:T(8,128)}, u32[]{:S(2)}) copy-start(f32[24,1024]{1,0:T(8,128)} %param.8) | copy-start | bytes 294916
  2.5 45.5 %all-to-all-start = ((bf16[8,128,128]{2,1,0:T(8,128)(2,1)}), bf16[8,128,128]{2,1,0:T(8,128)(2,1)S(1)}, u32[]{:S(2)}, u32[]{:S(2)}) async-start(bf16[8,128,128]{2,1,0:T(8,128)(2,1)} %bitcast.7), calls=%async_computation | async-start | bytes 524288 | tf_op jit(solution)/shard_map/all_to_all | solution.py:98
  9.9 0.7 copy-start.4
  43.4 1.0 copy-start.2
  47.9 12.6 %all-to-all-start.2 = ((bf16[8,128,128]{2,1,0:T(8,128)(2,1)}), bf16[8,128,128]{2,1,0:T(8,128)(2,1)S(1)}, u32[]{:S(2)}, u32[]{:S(2)}) async-start(bf16[8,128,128]{2,1,0:T(8,128)(2,1)} %bitcast.20), calls=%async_computation.2 | async-start | bytes 524288 | tf_op jit(solution)/shard_map/all_to_all | solution.py:108
  60.6 1.4 copy-start.1
  95.2 38.8 %collective-permute-start = (f32[24,128]{1,0:T(8,128)S(1)}, f32[24,128]{1,0:T(8,128)S(1)}, u32[]{:S(2)}, u32[]{:S(2)}) collective-permute-start(f32[24,128]{1,0:T(8,128)S(1)} %get-tuple-element.32), channel_id=1, source_target_pairs={{0,2},{2,4},{4,6},{6,8},{8,10},{10,12},{12,14},{14,0},{1,3},{3,5},... | collective-permute-start | bytes 36872 | tf_op jit(solution)/shard_map/ppermute | solution.py:19
  95.3 40.7 %collective-permute-start.1 = (f32[24,128]{1,0:T(8,128)S(1)}, f32[24,128]{1,0:T(8,128)S(1)}, u32[]{:S(2)}, u32[]{:S(2)}) collective-permute-start(f32[24,128]{1,0:T(8,128)S(1)} %get-tuple-element.32), channel_id=1, source_target_pairs={{0,14},{2,0},{4,2},{6,4},{8,6},{10,8},{12,10},{14,12},{1,15},{3,1}... | collective-permute-start | bytes 36872 | tf_op jit(solution)/shard_map/ppermute | solution.py:22
  130.6 24.9 %all-to-all-start.1 = ((bf16[128,8,128]{0,2,1:T(8,128)(2,1)}), bf16[128,8,128]{0,2,1:T(8,128)(2,1)S(1)}, u32[]{:S(2)}, u32[]{:S(2)}) async-start(bf16[128,8,128]{0,2,1:T(8,128)(2,1)} %bitcast.15), calls=%async_computation.1 | async-start | bytes 524288 | tf_op jit(solution)/shard_map/all_to_all | solution.py:123
  134.0 8.6 %collective-permute-start.2 = (f32[24,128]{1,0:T(8,128)S(1)}, f32[24,128]{1,0:T(8,128)S(1)}, u32[]{:S(2)}, u32[]{:S(2)}) collective-permute-start(f32[24,128]{1,0:T(8,128)S(1)} %collective-permute-done), channel_id=1, source_target_pairs={{0,2},{2,4},{4,6},{6,8},{8,10},{10,12},{12,14},{14,0},{1,3},{3,5},... | collective-permute-start | bytes 36872 | tf_op jit(solution)/shard_map/ppermute | solution.py:19
  136.0 6.7 %collective-permute-start.3 = (f32[24,128]{1,0:T(8,128)S(1)}, f32[24,128]{1,0:T(8,128)S(1)}, u32[]{:S(2)}, u32[]{:S(2)}) collective-permute-start(f32[24,128]{1,0:T(8,128)S(1)} %collective-permute-done.1), channel_id=1, source_target_pairs={{0,14},{2,0},{4,2},{6,4},{8,6},{10,8},{12,10},{14,12},{1,15},{3,1}... | collective-permute-start | bytes 36872 | tf_op jit(solution)/shard_map/ppermute | solution.py:22
  142.7 6.4 %collective-permute-start.4 = (f32[24,128]{1,0:T(8,128)S(1)}, f32[24,128]{1,0:T(8,128)S(1)}, u32[]{:S(2)}, u32[]{:S(2)}) collective-permute-start(f32[24,128]{1,0:T(8,128)S(1)} %collective-permute-done.2), channel_id=1, source_target_pairs={{0,2},{2,4},{4,6},{6,8},{8,10},{10,12},{12,14},{14,0},{1,3},{3,5},... | collective-permute-start | bytes 36872 | tf_op jit(solution)/shard_map/ppermute | solution.py:19
  142.7 6.4 %collective-permute-start.5 = (f32[24,128]{1,0:T(8,128)S(1)}, f32[24,128]{1,0:T(8,128)S(1)}, u32[]{:S(2)}, u32[]{:S(2)}) collective-permute-start(f32[24,128]{1,0:T(8,128)S(1)} %collective-permute-done.3), channel_id=1, source_target_pairs={{0,14},{2,0},{4,2},{6,4},{8,6},{10,8},{12,10},{14,12},{1,15},{3,1}... | collective-permute-start | bytes 36872 | tf_op jit(solution)/shard_map/ppermute | solution.py:22
  149.1 6.4 %collective-permute-start.6 = (f32[24,128]{1,0:T(8,128)S(1)}, f32[24,128]{1,0:T(8,128)S(1)}, u32[]{:S(2)}, u32[]{:S(2)}) collective-permute-start(f32[24,128]{1,0:T(8,128)S(1)} %collective-permute-done.4), channel_id=1, source_target_pairs={{0,2},{2,4},{4,6},{6,8},{8,10},{10,12},{12,14},{14,0},{1,3},{3,5},... | collective-permute-start | bytes 36872 | tf_op jit(solution)/shard_map/ppermute | solution.py:19
  155.5 0.6 copy-start.3
